TPU v7x, 32 devices: a whole 2x2x4 slice. The times are simulated.
32 devices in a mesh: child: 2 (over y), row: 4 (over x, core), col: 4 (over z).
Axes of the slice: x: 2, y: 2, z: 4, core: 2. Of those that a mesh axis runs over, the one named last changes fastest.
Arguments:
- child_blocks: float32 [2, 4096, 4096], P('child', 'row', 'col'), as said below
- child_panels: bfloat16 [2, 4096, 1024], P('child', 'row'), may hold values from -0.1875 to 0.1875
- child_patterns: int32 [2, 16, 16], replicated, may hold values from 0 to 1, as said below
- child_maps: int32 [2, 16], replicated, may hold values from 0 to 23, as said below
- parent_place: int32 [24], replicated, may hold values from 0 to 23, as said below
- parent_front: float32 [6144, 6144], P(('child', 'row'), 'col'), as said below
Outputs:
- factored: float32 [6144, 6144], P(('child', 'row'), 'col')
Inputs may be any that keep to these rules, and one draw needn't show every extreme that they name: `parent_place`: a permutation. The entries of one child are distinct; within each aligned block of 4 entries of one child, the values parent_place[child_maps[c, i]] // 6 are distinct. `child_patterns`: symmetric in its two tile dimensions, with ones on the diagonal. `child_blocks`: each child's block is symmetric. `parent_front`: symmetric; the diagonal entries inside stored tiles (parent_place[0], parent_place[0]) and (parent_place[1], parent_place[1]) lie between 200 and 400.
All inputs are finite; a program needn't handle non-finite values.
Results may differ from a plain program's by a relative error of at most 0.0003.
Values may be sent and summed in bfloat16 or wider, within the bound.
A program may use at most 128 MiB of HBM per device.

v0:
```python
import jax
import jax.numpy as jnp
from jax import lax
from jax.sharding import PartitionSpec as P

TILE = 256
PANEL = 512


def spread(block, axis, source):
    block = jnp.where(lax.axis_index(axis) == source, block, jnp.zeros_like(block))
    return lax.psum(block, axis)


def lookup(lookup_table, positions):
    matches = positions[:, None] == jnp.arange(lookup_table.shape[0], dtype=jnp.int32)[None, :]
    return jnp.sum(jnp.where(matches, lookup_table[None, :], 0), axis=1)


def find_owner(slot_list, targets):
    matches = targets[:, None] == slot_list[None, :]
    located = jnp.any(matches, axis=1)
    chosen = jnp.sum(
        jnp.where(matches, jnp.arange(slot_list.shape[0], dtype=jnp.int32)[None, :], 0), axis=1
    )
    return (located, chosen)


def select_tiles(source, located, chosen, axis_pos):
    selected = jnp.take(source, chosen, axis=axis_pos)
    dims_shape = [1] * source.ndim
    dims_shape[axis_pos] = located.shape[0]
    return jnp.where(located.reshape(dims_shape), selected, jnp.zeros((), source.dtype))


def body(child_blocks, child_panels, child_patterns, child_maps, parent_place, parent_front):
    child_index = lax.axis_index("child")
    row_index = lax.axis_index("row")
    col_index = lax.axis_index("col")
    row_count = lax.axis_size("row")
    col_count = lax.axis_size("col")
    group_count = lax.axis_size(("child", "row"))
    own_block = child_blocks[0]
    block_width = own_block.shape[0]
    tiles_dev = block_width // TILE
    rows_dev = parent_front.shape[0] // TILE
    cols_dev = parent_front.shape[1] // TILE
    own_panel = child_panels[0]
    partner = spread(own_panel, "row", col_index)
    product = lax.dot_general(
        own_panel, partner, (((1,), (1,)), ((), ())), preferred_element_type=jnp.float32
    )
    pattern = lax.dynamic_index_in_dim(child_patterns, child_index, 0, keepdims=False)
    pattern = lax.dynamic_slice(
        pattern, (row_index * tiles_dev, col_index * tiles_dev), (tiles_dev, tiles_dev)
    ).astype(jnp.float32)
    update = (own_block - product).reshape(tiles_dev, TILE, tiles_dev, TILE) * pattern[
        :, None, :, None
    ]
    slot_table = jnp.stack(
        [lookup(parent_place, child_maps[0]), lookup(parent_place, child_maps[1])]
    )
    own_slots = lax.dynamic_index_in_dim(slot_table, child_index, 0, keepdims=False)
    row_slots = lax.dynamic_slice_in_dim(own_slots, row_index * tiles_dev, tiles_dev)
    col_slots = lax.dynamic_slice_in_dim(own_slots, col_index * tiles_dev, tiles_dev)
    group_index = child_index * row_count + row_index
    row_targets = group_index * rows_dev + jnp.arange(rows_dev, dtype=jnp.int32)
    col_targets = col_index * cols_dev + jnp.arange(cols_dev, dtype=jnp.int32)
    group_ids = jnp.arange(group_count, dtype=jnp.int32)
    column_ids = jnp.arange(col_count, dtype=jnp.int32)
    located, chosen = find_owner(col_slots // cols_dev, column_ids)
    outgoing = select_tiles(update.reshape(block_width, tiles_dev, TILE), located, chosen, 1)
    incoming = lax.all_to_all(outgoing, "col", split_axis=1, concat_axis=1, tiled=True)
    located, chosen = find_owner(own_slots, col_targets)
    placed = select_tiles(incoming, located, chosen // tiles_dev, 1).reshape(
        tiles_dev, TILE, cols_dev * TILE
    )
    located, chosen = find_owner(row_slots // rows_dev, group_ids)
    outgoing_rows = select_tiles(placed, located, chosen, 0)
    incoming_rows = lax.all_to_all(
        outgoing_rows, ("child", "row"), split_axis=0, concat_axis=0, tiled=True
    )
    contribution = jnp.zeros((rows_dev, TILE, cols_dev * TILE), jnp.float32)
    for member in range(2):
        located, chosen = find_owner(slot_table[member], row_targets)
        sender = member * row_count + chosen // tiles_dev
        contribution = contribution + select_tiles(incoming_rows, located, sender, 0)
    assembled = parent_front + contribution.reshape(parent_front.shape)
    panel_slots = parent_place[0:2]
    col_local = panel_slots // cols_dev == col_index
    col_pos = panel_slots % cols_dev
    row_local = panel_slots // rows_dev == group_index
    row_pos = panel_slots % rows_dev
    front_tiles = assembled.reshape(rows_dev * TILE, cols_dev, TILE)
    column = select_tiles(front_tiles, col_local, col_pos, 1).reshape(rows_dev * TILE, PANEL)
    diagonal_part = select_tiles(
        column.reshape(rows_dev, TILE, PANEL), row_local, row_pos, 0
    ).reshape(PANEL, PANEL)
    panel_column = lax.psum(column, "col")
    diagonal_block = lax.psum(diagonal_part, ("child", "row", "col"))
    factor = jnp.linalg.cholesky(diagonal_block)
    panel_rows = lax.linalg.triangular_solve(
        factor, panel_column, left_side=False, lower=True, transpose_a=True
    )
    halves = []
    for member in range(2):
        halves.append(spread(panel_rows, ("child", "row"), 2 * col_index + member))
    panel_cols = jnp.concatenate(halves, axis=0)
    result = assembled - lax.dot_general(
        panel_rows,
        panel_cols,
        (((1,), (1,)), ((), ())),
        precision=lax.Precision.HIGHEST,
        preferred_element_type=jnp.float32,
    )
    result_tiles = result.reshape(rows_dev * TILE, cols_dev, TILE)
    tile_positions = jnp.arange(cols_dev, dtype=jnp.int32)
    for member in range(2):
        chosen_cols = jnp.logical_and(tile_positions == col_pos[member], col_local[member])
        result_tiles = jnp.where(
            chosen_cols[None, :, None],
            panel_rows[:, None, member * TILE : (member + 1) * TILE],
            result_tiles,
        )
    return result_tiles.reshape(parent_front.shape)


def solution(mesh):
    return jax.shard_map(
        body,
        mesh=mesh,
        in_specs=(
            P("child", "row", "col"),
            P("child", "row", None),
            P(),
            P(),
            P(),
            P(("child", "row"), "col"),
        ),
        out_specs=P(("child", "row"), "col"),
        check_vma=False,
    )
```

profile of v0, /device:TPU:0, one launch (start us, length us, event | category | flops | bytes accessed | tf_op | source)
XLA Modules:
  0.0 784.7 jit_solution(8666867808019406183)
XLA Ops:
  6.5 3.0 bitcast_select_fusion
  9.7 0.8 convert_bitcast_fusion
  10.8 5.5 copy.61
  16.7 47.2 %all-reduce.7.cloned.1.call-done = bf16[1024,1024]{1,0:T(8,128)(2,1)} async-done(((bf16[1024,1024]{1,0:T(8,128)(2,1)}), bf16[1024,1024]{1,0:T(8,128)(2,1)}) %all-reduce.7.cloned.1.call-update) | async-done | bytes 2097168 | tf_op jit(solution)/shard_map/psum | solution.py:12
  63.9 5.2 bitcast_subtract_fusion
  69.1 2.5 broadcast_multiply_fusion
  71.6 4.9 gather_fusion
  76.5 5.2 select_bitcast_fusion
  81.7 4.9 all-to-all-start
  87.4 92.4 %all-to-all-done = f32[1024,4,256]{0,2,1:T(8,128)} async-done(((f32[1024,4,256]{0,2,1:T(8,128)}), f32[1024,4,256]{0,2,1:T(8,128)}, u32[]{:S(2)}, u32[]{:S(2)}) %all-to-all-start) | async-done | bytes 4194336 | tf_op jit(solution)/shard_map/all_to_all | solution.py:73
  179.8 5.8 gather_fusion.1
  185.6 8.1 %gather.35 = f32[4,256,1536]{1,0,2:T(4,128)} reshape(f32[1024,6,256]{0,2,1:T(8,128)} %bitcast.115) | data formatting | bytes 12582912 | tf_op jit(solution)/shard_map/jit(_take)/gather | solution.py:30
  193.7 7.6 copy.63
  201.3 6.3 select_select_fusion.1
  207.6 8.6 %gather_fusion.2 = f32[8,256,1536]{2,1,0:T(8,128)} fusion(f32[4,256,1536]{2,1,0:T(8,128)} %select_select_fusion.1, s32[1024]{0:T(1024)S(1)} %pad_clamp_fusion.4), kind=kCustom, calls=%fused_computation.4 | custom fusion | bytes 25165856 | tf_op jit(solution)/shard_map/jit(_take)/gather | solution.py:30
  216.2 11.4 %select_select_fusion = f32[8,256,1536]{2,1,0:T(8,128)} fusion(f32[8,256,1536]{2,1,0:T(8,128)} %gather_fusion.2, pred[8]{0:T(512)(128)(4,1)S(1)} %compare_and_fusion.6, pred[8]{0:T(512)(128)(4,1)S(1)} %fusion.35), kind=kLoop, calls=%fused_computation.9 | loop fusion | flops 6291456 | bytes 25165840 | tf_op jit(solution)/shard_map/jit(_where)/select_n | solution.py:33
  227.6 5.3 all-to-all-start.1
  234.1 137.9 %all-to-all-done.1 = f32[8,256,1536]{2,1,0:T(8,128)} async-done(((f32[8,256,1536]{2,1,0:T(8,128)}), f32[8,256,1536]{2,1,0:T(8,128)}, u32[]{:S(2)}, u32[]{:S(2)}) %all-to-all-start.1) | async-done | bytes 12582944 | tf_op jit(solution)/shard_map/all_to_all | solution.py:80
  372.0 7.5 gather_fusion.5
  379.5 7.7 gather_fusion.6
  387.2 5.1 fusion
  392.3 3.2 bitcast_add_fusion
  395.5 6.0 copy.64
  401.6 6.1 copy.65
  407.7 3.0 gather_fusion.3
  410.7 2.4 copy.67
  413.1 2.5 gather.39
  415.6 1.4 select_select_fusion.5
  417.0 2.0 gather_fusion.4
  419.0 1.3 copy.88
  420.3 2.3 select_select_fusion.7
  423.3 1.4 fusion.5
  424.9 125.9 %all-reduce.11.cloned.1.call-done = f32[512,512]{0,1:T(8,128)} async-done(((f32[512,512]{0,1:T(8,128)}), f32[512,512]{0,1:T(8,128)}) %all-reduce.11.cloned.1.call-update) | async-done | bytes 1048592 | tf_op jit(solution)/shard_map/psum | solution.py:100
  550.8 1.6 copy.69
  552.3 1.4 fusion.11
  553.8 11.7 %cholesky.102 = f32[128,128]{1,0:T(8,128)S(1)} custom-call(f32[128,128]{1,0:T(8,128)S(1)} %cholesky.260), custom_call_target="Cholesky" | custom-call | tf_op jit(solution)/shard_map/jit(cholesky)/cholesky | solution.py:101
  565.6 9.8 %custom-call.30 = f32[1,128,128]{1,2,0:T(8,128)S(1)} custom-call(f32[1,128,128]{2,1,0:T(8,128)S(1)} %get-tuple-element.63), custom_call_target="InvertDiagBlocksLowerTriangular" | custom-call | tf_op jit(solution)/shard_map/jit(cholesky)/cholesky | solution.py:101
  576.0 11.7 %cholesky.213 = f32[128,128]{1,0:T(8,128)S(1)} custom-call(f32[128,128]{1,0:T(8,128)S(1)} %cholesky.264), custom_call_target="Cholesky" | custom-call | tf_op jit(solution)/shard_map/jit(cholesky)/cholesky | solution.py:101
  588.1 10.2 %custom-call.31 = f32[1,128,128]{1,2,0:T(8,128)S(1)} custom-call(f32[1,128,128]{2,1,0:T(8,128)S(1)} %get-tuple-element.61), custom_call_target="InvertDiagBlocksLowerTriangular" | custom-call | tf_op jit(solution)/shard_map/jit(cholesky)/cholesky | solution.py:101
  599.4 11.7 %cholesky.234 = f32[128,128]{1,0:T(8,128)S(1)} custom-call(f32[128,128]{1,0:T(8,128)S(1)} %cholesky.269), custom_call_target="Cholesky" | custom-call | tf_op jit(solution)/shard_map/jit(cholesky)/cholesky | solution.py:101
  611.3 9.8 %custom-call.32 = f32[1,128,128]{1,2,0:T(8,128)S(1)} custom-call(f32[1,128,128]{2,1,0:T(8,128)S(1)} %get-tuple-element.59), custom_call_target="InvertDiagBlocksLowerTriangular" | custom-call | tf_op jit(solution)/shard_map/jit(cholesky)/cholesky | solution.py:101
  621.9 11.8 %cholesky.251 = f32[128,128]{1,0:T(8,128)S(1)} custom-call(f32[128,128]{1,0:T(8,128)S(1)} %convolution_subtract_fusion.5), custom_call_target="Cholesky" | custom-call | tf_op jit(solution)/shard_map/jit(cholesky)/cholesky | solution.py:101
  633.9 0.7 compare_reduce_fusion.5
  635.1 0.7 compare_reduce_fusion.4
  639.1 8.0 %while.1 = (s32[]{:T(128)}, f32[512,512]{0,1:T(8,128)S(1)}, s32[4,2]{0,1:T(2,128)S(1)}, f32[4,128,128]{2,1,0:T(8,128)S(1)}, s32[]{:T(128)}) while((s32[]{:T(128)}, f32[512,512]{0,1:T(8,128)S(1)}, s32[4,2]{0,1:T(2,128)S(1)}, f32[4,128,128]{2,1,0:T(8,128)S(1)}, s32[]{:T(128)}) %tuple.46), condition=%wide.while_cond, body=%wide.while_body.sunk | while | flops 2 | bytes 393321 | solution.py:102
  639.7 1.3 dynamic-slice.10
  641.7 1.3 dynamic-slice.10
  643.7 1.3 dynamic-slice.10
  645.6 1.3 dynamic-slice.10
  647.0 39.3 %custom-call.33 = f32[4,128,128]{1,2,0:T(8,128)S(1)} custom-call(f32[4,128,128]{2,1,0:T(8,128)S(1)} %get-tuple-element.13), custom_call_target="InvertDiagBlocksLowerTriangular" | custom-call | tf_op jit(solution)/shard_map/triangular_solve | solution.py:102
  686.4 1.5 fusion.12
  687.9 1.5 convolution_subtract_fusion.1
  690.0 1.6 convolution_subtract_fusion.2
  692.1 1.9 convolution_subtract_fusion
  694.6 1.8 broadcast_select_fusion.1
  697.1 0.6 fusion.47
  697.7 1.3 compare_and_fusion.8
  699.1 1.3 compare_and_fusion.2
  700.5 2.6 broadcast_in_dim.369
  703.1 6.1 copy.81
  709.2 2.6 broadcast_in_dim.364
  711.8 6.2 copy.82
  718.0 46.9 %all-reduce.13.cloned.1.call-done = (f32[768,512]{0,1:T(8,128)}, f32[768,512]{0,1:T(8,128)}) async-done(((f32[768,512]{0,1:T(8,128)}, f32[768,512]{0,1:T(8,128)}), (f32[768,512]{0,1:T(8,128)}, f32[768,512]{0,1:T(8,128)})) %all-reduce.13.cloned.1.call-update) | async-done | bytes 3145744 | tf_op jit(solution)/shard_map/psum | solution.py:12
  764.9 13.1 %select_select_fusion.4 = f32[768,1536]{1,0:T(8,128)} fusion(f32[768,1536]{1,0:T(8,128)} %copy.82, f32[768,1536]{1,0:T(8,128)} %copy.81, f32[768,1536]{1,0:T(8,128)} %bitcast_add_fusion, f32[768,512]{0,1:T(8,128)} %get-tuple-element.44, f32[768,512]{0,1:T(8,128)} %get-tuple-element.45, pred[1536]{0:T(1024)(128)(4,1)S(1)} %broadcast_in_dim.367, ...), kind=kOutput, calls=%fused_computation.15 | convolution fusion | flops 7253262336 | bytes 23596032 | tf_op jit(solution)/shard_map/dot_general | solution.py:109
  (122 shorter events, 13.2 us)
Async XLA Ops:
  6.5 3.1 copy-start.2
  6.5 4.1 copy-start.1
  6.5 57.3 %all-reduce.7.cloned.1.call-start = ((), (), s32[]{:S(2)}) async-start(), calls=%async_computation.2 | async-start | bytes 4194304 | tf_op jit(solution)/shard_map/psum | solution.py:12
  10.8 53.1 %copy-start = (bf16[1,1024,1024]{2,1,0:T(8,128)(2,1)S(1)}, bf16[1,1024,1024]{2,1,0:T(8,128)(2,1)}, u32[]{:S(2)}) copy-start(bf16[1,1024,1024]{2,1,0:T(8,128)(2,1)} %param.9) | copy-start | bytes 6291460
  81.7 98.1 %all-to-all-start = ((f32[1024,4,256]{0,2,1:T(8,128)}), f32[1024,4,256]{0,2,1:T(8,128)}, u32[]{:S(2)}, u32[]{:S(2)}) async-start(f32[1024,4,256]{0,2,1:T(8,128)} %select_bitcast_fusion), calls=%async_computation | async-start | bytes 8388608 | tf_op jit(solution)/shard_map/all_to_all | solution.py:73
  227.6 144.3 %all-to-all-start.1 = ((f32[8,256,1536]{2,1,0:T(8,128)}), f32[8,256,1536]{2,1,0:T(8,128)}, u32[]{:S(2)}, u32[]{:S(2)}) async-start(f32[8,256,1536]{2,1,0:T(8,128)} %select_select_fusion), calls=%async_computation.1 | async-start | bytes 25165824 | tf_op jit(solution)/shard_map/all_to_all | solution.py:80
  233.0 317.8 %all-reduce.11.cloned.1.call-start = ((), (), s32[]{:S(2)}) async-start(), calls=%async_computation.4 | async-start | bytes 2097152 | tf_op jit(solution)/shard_map/psum | solution.py:100
  379.5 12.8 %slice-start = ((s8[4718592]{0:T(1024)(128)(4,1)}), s8[524288]{0:T(1024)(128)(4,1)S(1)}, s32[]{:S(2)}) async-start(s8[4718592]{0:T(1024)(128)(4,1)} %bitcast.121), calls=%async_computation.6 | async-start | bytes 1048576
  387.2 5.1 slice-start.1
  422.7 263.7 %all-reduce.9.cloned.1.call-start = ((), (), s32[]{:S(2)}) async-start(), calls=%async_computation.3 | async-start | bytes 3145728 | tf_op jit(solution)/shard_map/psum | solution.py:99
  424.7 340.2 %all-reduce.13.cloned.1.call-start = ((), (), s32[]{:S(2)}) async-start(), calls=%async_computation.5 | async-start | bytes 6291456 | tf_op jit(solution)/shard_map/psum | solution.py:12
Sparse Core Ops, SparseCore 0:
  9.7 54.0 all-reduce.6
  422.8 127.9 all-reduce.10
  553.2 67.9 all-reduce.8
  696.6 68.2 all-reduce.12
where the time goes:
time: 793 us; the launch traced here: 785 us
  waiting for transfers between devices  450 us (57%)
  other arithmetic  169 us (21%)
  local copies, waits for them, and re-layouts  109 us (14%)
  matrix products  28.8 us (4%)
  between operations  16.3 us (2%)
  starting transfers between devices  10.7 us (1%)
    all_to_all x1, waiting for transfers between devices, body(): lax.all_to_all(outgoing_rows, ('child', 'row'), split_axis=0, concat_axis...  138 us
    psum x1, waiting for transfers between devices, body(): diagonal_block = lax.psum(diagonal_part, ('child', 'row', 'col'))  126 us
    psum x2, waiting for transfers between devices, spread(): return lax.psum(block, axis)  94.1 us
    all_to_all x1, waiting for transfers between devices, body(): lax.all_to_all(outgoing, 'col', split_axis=1, concat_axis=1, tiled=True)  92.4 us
    another operation x15, other arithmetic, body(): factor = jnp.linalg.cholesky(diagonal_block)  79.5 us
    gather x13, local copies, waits for them, and re-layouts, select_tiles(): selected = jnp.take(source, chosen, axis=axis_pos)  61.9 us
    another operation x5, other arithmetic, body(): lax.linalg.triangular_solve(factor, panel_column, left_side=False, lower=...  39.6 us
    select_n x6, other arithmetic, select_tiles(): jnp.where(located.reshape(dims_shape), selected, jnp.zeros((), source.dty...  28 us
  transfers between devices with their start and end apart: 6, of which 5 were waited for; matrix products, arithmetic and copies ran while one was open for 21% of the time, Pallas kernels for 0%

commit v1 on v0

--- a/solution.py
+++ b/solution.py
@@ -9,7 +9,7 @@
 
 def spread(block, axis, source):
     block = jnp.where(lax.axis_index(axis) == source, block, jnp.zeros_like(block))
-    return lax.psum(block, axis)
+    return jnp.sum(lax.all_gather(block, axis), axis=0)
 
 
 def lookup(lookup_table, positions):

time: 793 us -> 901 us (1.14)
  waiting for transfers between devices: 450 us -> 522 us
  other arithmetic: 169 us -> 192 us
  local copies, waits for them, and re-layouts: 109 us -> 122 us
    all_gather x0 -> x3, waiting for transfers between devices: none -> 166 us  [spread(): return jnp.sum(lax.all_gather(block, axis), axis=0)]
    psum x2 -> x0, waiting for transfers between devices: 94.1 us -> none  [spread(): return lax.psum(block, axis)]
    reduce_sum x0 -> x3, other arithmetic: none -> 22.5 us  [spread(): return jnp.sum(lax.all_gather(block, axis), axis=0)]
    gather x13 -> x14, local copies, waits for them, and re-layouts: 61.9 us -> 62.4 us  [select_tiles(): selected = jnp.take(source, chosen, axis=axis_pos)]
  transfers between devices with their start and end apart: 6 -> 7, of which waited for: 5 -> 6; matrix products, arithmetic and copies ran while one was open for 21% -> 20% of each run, Pallas kernels for 0% -> 0%
where the time goes in v1:
time: 901 us; the launch traced here: 894 us
  waiting for transfers between devices  522 us (58%)
  other arithmetic  192 us (21%)
  local copies, waits for them, and re-layouts  122 us (14%)
  matrix products  30.5 us (3%)
  between operations  16.6 us (2%)
  starting transfers between devices  11.6 us (1%)
    all_gather x3, waiting for transfers between devices, spread(): return jnp.sum(lax.all_gather(block, axis), axis=0)  166 us
    all_to_all x1, waiting for transfers between devices, body(): lax.all_to_all(outgoing_rows, ('child', 'row'), split_axis=0, concat_axis...  138 us
    psum x1, waiting for transfers between devices, body(): diagonal_block = lax.psum(diagonal_part, ('child', 'row', 'col'))  125 us
    all_to_all x1, waiting for transfers between devices, body(): lax.all_to_all(outgoing, 'col', split_axis=1, concat_axis=1, tiled=True)  93.1 us
    another operation x15, other arithmetic, body(): factor = jnp.linalg.cholesky(diagonal_block)  79.3 us
    gather x14, local copies, waits for them, and re-layouts, select_tiles(): selected = jnp.take(source, chosen, axis=axis_pos)  62.4 us
    another operation x5, other arithmetic, body(): lax.linalg.triangular_solve(factor, panel_column, left_side=False, lower=...  40.4 us
    select_n x6, other arithmetic, select_tiles(): jnp.where(located.reshape(dims_shape), selected, jnp.zeros((), source.dty...  28 us
  transfers between devices with their start and end apart: 7, of which 6 were waited for; matrix products, arithmetic and copies ran while one was open for 20% of the time, Pallas kernels for 0%

profile of v1, /device:TPU:0, one launch (start us, length us, event | category | flops | bytes accessed | tf_op | source)
XLA Modules:
  0.0 894.1 jit_solution(2117459967158461599)
XLA Ops:
  6.5 3.1 broadcast_select_fusion
  10.7 5.4 copy.81
  16.6 53.7 %all-gather.4.cloned.1.call-done = bf16[4,1024,1024]{2,1,0:T(8,128)(2,1)} async-done(((bf16[1,1024,1024]{2,1,0:T(8,128)(2,1)}), bf16[4,1024,1024]{2,1,0:T(8,128)(2,1)}) %all-gather.4.cloned.1.call-update) | async-done | bytes 8388624 | tf_op jit(solution)/shard_map/all_gather | solution.py:12
  70.4 7.5 reduce_sum.104
  77.9 5.2 bitcast_subtract_fusion
  83.1 2.5 broadcast_multiply_fusion
  85.6 4.9 gather_fusion
  90.5 5.2 select_bitcast_fusion
  95.7 5.1 all-to-all-start
  101.6 93.1 %all-to-all-done = f32[1024,4,256]{0,2,1:T(8,128)} async-done(((f32[1024,4,256]{0,2,1:T(8,128)}), f32[1024,4,256]{0,2,1:T(8,128)}, u32[]{:S(2)}, u32[]{:S(2)}) %all-to-all-start) | async-done | bytes 4194336 | tf_op jit(solution)/shard_map/all_to_all | solution.py:73
  194.7 5.8 gather_fusion.1
  200.5 8.1 gather.35
  208.5 7.6 copy.83
  216.2 6.3 select_select_fusion.1
  222.4 8.6 gather_fusion.2
  231.0 11.4 %select_select_fusion = f32[8,256,1536]{2,1,0:T(8,128)} fusion(f32[8,256,1536]{2,1,0:T(8,128)} %gather_fusion.2, pred[8]{0:T(512)(128)(4,1)S(1)} %compare_and_fusion.6, pred[8]{0:T(512)(128)(4,1)S(1)} %fusion.43), kind=kLoop, calls=%fused_computation.9 | loop fusion | flops 6291456 | bytes 25165840 | tf_op jit(solution)/shard_map/jit(_where)/select_n | solution.py:33
  242.5 5.3 all-to-all-start.1
  249.0 137.8 %all-to-all-done.1 = f32[8,256,1536]{2,1,0:T(8,128)} async-done(((f32[8,256,1536]{2,1,0:T(8,128)}), f32[8,256,1536]{2,1,0:T(8,128)}, u32[]{:S(2)}, u32[]{:S(2)}) %all-to-all-start.1) | async-done | bytes 12582944 | tf_op jit(solution)/shard_map/all_to_all | solution.py:80
  386.8 7.5 gather_fusion.5
  394.4 7.7 gather_fusion.6
  402.0 5.1 fusion
  407.2 3.2 bitcast_add_fusion
  410.4 6.0 copy.84
  416.4 6.1 copy.85
  422.6 3.0 gather_fusion.3
  425.6 2.4 copy.88
  427.9 2.5 gather.39
  430.5 1.4 select_select_fusion.5
  431.9 2.0 gather_fusion.4
  433.9 1.3 copy.107
  435.2 2.3 select_select_fusion.8
  438.6 1.3 select_select_fusion.6
  440.5 125.1 %all-reduce.6.cloned.1.call-done = f32[512,512]{0,1:T(8,128)} async-done(((f32[512,512]{0,1:T(8,128)}), f32[512,512]{0,1:T(8,128)}) %all-reduce.6.cloned.1.call-update) | async-done | bytes 1048592 | tf_op jit(solution)/shard_map/psum | solution.py:100
  565.6 1.6 copy.90
  567.2 1.4 fusion.17
  568.6 11.7 %cholesky.102 = f32[128,128]{1,0:T(8,128)S(1)} custom-call(f32[128,128]{1,0:T(8,128)S(1)} %cholesky.260), custom_call_target="Cholesky" | custom-call | tf_op jit(solution)/shard_map/jit(cholesky)/cholesky | solution.py:101
  580.4 9.8 %custom-call.30 = f32[1,128,128]{1,2,0:T(8,128)S(1)} custom-call(f32[1,128,128]{2,1,0:T(8,128)S(1)} %get-tuple-element.65), custom_call_target="InvertDiagBlocksLowerTriangular" | custom-call | tf_op jit(solution)/shard_map/jit(cholesky)/cholesky | solution.py:101
  590.9 11.7 %cholesky.213 = f32[128,128]{1,0:T(8,128)S(1)} custom-call(f32[128,128]{1,0:T(8,128)S(1)} %cholesky.264), custom_call_target="Cholesky" | custom-call | tf_op jit(solution)/shard_map/jit(cholesky)/cholesky | solution.py:101
  602.9 9.9 %custom-call.31 = f32[1,128,128]{1,2,0:T(8,128)S(1)} custom-call(f32[1,128,128]{2,1,0:T(8,128)S(1)} %get-tuple-element.63), custom_call_target="InvertDiagBlocksLowerTriangular" | custom-call | tf_op jit(solution)/shard_map/jit(cholesky)/cholesky | solution.py:101
  614.0 11.7 %cholesky.234 = f32[128,128]{1,0:T(8,128)S(1)} custom-call(f32[128,128]{1,0:T(8,128)S(1)} %cholesky.269), custom_call_target="Cholesky" | custom-call | tf_op jit(solution)/shard_map/jit(cholesky)/cholesky | solution.py:101
  625.9 9.8 %custom-call.32 = f32[1,128,128]{1,2,0:T(8,128)S(1)} custom-call(f32[1,128,128]{2,1,0:T(8,128)S(1)} %get-tuple-element.61), custom_call_target="InvertDiagBlocksLowerTriangular" | custom-call | tf_op jit(solution)/shard_map/jit(cholesky)/cholesky | solution.py:101
  636.5 11.9 %cholesky.251 = f32[128,128]{1,0:T(8,128)S(1)} custom-call(f32[128,128]{1,0:T(8,128)S(1)} %convolution_subtract_fusion.5), custom_call_target="Cholesky" | custom-call | tf_op jit(solution)/shard_map/jit(cholesky)/cholesky | solution.py:101
  653.7 10.3 %while.1 = (s32[]{:T(128)}, f32[512,512]{0,1:T(8,128)S(1)}, s32[4,2]{0,1:T(2,128)S(1)}, f32[4,128,128]{2,1,0:T(8,128)}, s32[]{:T(128)}) while((s32[]{:T(128)}, f32[512,512]{0,1:T(8,128)S(1)}, s32[4,2]{0,1:T(2,128)S(1)}, f32[4,128,128]{2,1,0:T(8,128)}, s32[]{:T(128)}) %tuple.47), condition=%wide.while_cond, body=%wide.while_body.sunk | while | flops 2 | bytes 393829 | solution.py:102
  654.3 1.3 dynamic-slice.10
  662.0 1.3 dynamic-slice.10
  664.0 40.1 %custom-call.33 = f32[4,128,128]{1,2,0:T(8,128)S(1)} custom-call(f32[4,128,128]{2,1,0:T(8,128)} %get-tuple-element.13), custom_call_target="InvertDiagBlocksLowerTriangular" | custom-call | tf_op jit(solution)/shard_map/triangular_solve | solution.py:102
  704.2 1.5 fusion.20
  705.7 1.8 convolution_subtract_fusion.1
  708.0 2.4 convolution_subtract_fusion.2
  711.0 3.1 convolution_subtract_fusion
  714.6 1.4 fusion.19
  715.9 3.1 copy.99
  719.3 1.6 copy.101
  724.8 2.6 broadcast_in_dim.369
  727.4 6.4 copy.103
  733.9 2.6 broadcast_in_dim.364
  736.5 6.0 copy.104
  742.5 47.6 %all-gather.6.cloned.1.call-done = f32[8,768,512]{2,1,0:T(8,128)} async-done(((f32[1,768,512]{2,1,0:T(8,128)}), f32[8,768,512]{2,1,0:T(8,128)}) %all-gather.6.cloned.1.call-update) | async-done | bytes 12582928 | tf_op jit(solution)/shard_map/all_gather | solution.py:12
  790.1 7.5 reduce_sum.110
  797.6 2.1 copy.109
  799.7 64.2 %all-gather.8.cloned.1.call-done = f32[8,768,512]{2,1,0:T(8,128)} async-done(((f32[1,768,512]{2,1,0:T(8,128)}), f32[8,768,512]{2,1,0:T(8,128)}) %all-gather.8.cloned.1.call-update) | async-done | bytes 12582928 | tf_op jit(solution)/shard_map/all_gather | solution.py:12
  863.9 7.5 reduce_sum.111
  871.4 3.0 copy.110
  874.4 12.7 %select_select_fusion.4 = f32[768,1536]{1,0:T(8,128)} fusion(f32[768,1536]{1,0:T(8,128)} %copy.104, f32[768,1536]{1,0:T(8,128)} %copy.103, f32[768,1536]{1,0:T(8,128)} %bitcast_add_fusion, f32[768,512]{0,1:T(8,128)} %copy.110, f32[768,512]{0,1:T(8,128)S(1)} %copy.109, pred[1536]{0:T(1024)(128)(4,1)S(1)} %broadcast_in_dim.367, ...), kind=kOutput, calls=%fused_computation.15 | convolution fusion | flops 7253262336 | bytes 23596032 | tf_op jit(solution)/shard_map/dot_general | solution.py:109
  (133 shorter events, 24.4 us)
Async XLA Ops:
  6.5 63.8 %all-gather.4.cloned.1.call-start = ((), (), s32[]{:S(2)}) async-start(), calls=%async_computation.2 | async-start | bytes 10485760 | tf_op jit(solution)/shard_map/all_gather | solution.py:12
  10.7 5.4 copy-start.2
  10.7 5.4 copy-start.1
  16.6 61.3 %copy-start = (bf16[1,1024,1024]{2,1,0:T(8,128)(2,1)S(1)}, bf16[1,1024,1024]{2,1,0:T(8,128)(2,1)}, u32[]{:S(2)}) copy-start(bf16[1,1024,1024]{2,1,0:T(8,128)(2,1)} %param.9) | copy-start | bytes 6291460
  95.7 99.0 %all-to-all-start = ((f32[1024,4,256]{0,2,1:T(8,128)}), f32[1024,4,256]{0,2,1:T(8,128)}, u32[]{:S(2)}, u32[]{:S(2)}) async-start(f32[1024,4,256]{0,2,1:T(8,128)} %select_bitcast_fusion), calls=%async_computation | async-start | bytes 8388608 | tf_op jit(solution)/shard_map/all_to_all | solution.py:73
  242.5 144.3 %all-to-all-start.1 = ((f32[8,256,1536]{2,1,0:T(8,128)}), f32[8,256,1536]{2,1,0:T(8,128)}, u32[]{:S(2)}, u32[]{:S(2)}) async-start(f32[8,256,1536]{2,1,0:T(8,128)} %select_select_fusion), calls=%async_computation.1 | async-start | bytes 25165824 | tf_op jit(solution)/shard_map/all_to_all | solution.py:80
  247.8 317.8 %all-reduce.6.cloned.1.call-start = ((), (), s32[]{:S(2)}) async-start(), calls=%async_computation.4 | async-start | bytes 2097152 | tf_op jit(solution)/shard_map/psum | solution.py:100
  394.4 12.8 %slice-start = ((s8[4718592]{0:T(1024)(128)(4,1)}), s8[524288]{0:T(1024)(128)(4,1)S(1)}, s32[]{:S(2)}) async-start(s8[4718592]{0:T(1024)(128)(4,1)} %bitcast.126), calls=%async_computation.7 | async-start | bytes 1048576
  402.0 5.1 slice-start.1
  437.6 266.6 %all-reduce.4.cloned.1.call-start = ((), (), s32[]{:S(2)}) async-start(), calls=%async_computation.3 | async-start | bytes 3145728 | tf_op jit(solution)/shard_map/psum | solution.py:99
  440.0 350.2 %all-gather.6.cloned.1.call-start = ((), (), s32[]{:S(2)}) async-start(), calls=%async_computation.5 | async-start | bytes 14155776 | tf_op jit(solution)/shard_map/all_gather | solution.py:12
  719.0 144.9 %all-gather.8.cloned.1.call-start = ((), (), s32[]{:S(2)}) async-start(), calls=%async_computation.6 | async-start | bytes 14155776 | tf_op jit(solution)/shard_map/all_gather | solution.py:12
Sparse Core Ops, SparseCore 0:
  9.8 60.5 all-gather.3
  437.7 127.8 all-reduce.5
  568.0 68.1 all-reduce.3
  719.2 70.9 all-gather.5
  791.9 71.9 all-gather.7
